TPU v7x, 128 devices: a whole 4x4x4 slice. The times are simulated.
128 devices in a mesh: lat: 8 (over y, z_lo), lon: 16 (over z_hi, x, core).
Axes of the slice: x: 4, y: 4, z: 4 (z_hi: 2, z_lo: 2; z = z_hi * 2 + z_lo), core: 2. Of those that a mesh axis runs over, the one named last changes fastest.
Arguments:
- state: bfloat16 [1024, 2048, 128], P('lat', 'lon'), may hold values from -6 to 6
- edge_metric: float32 [9, 1024, 2048], P(None, 'lat', 'lon'), may hold values from 0.1 to 1
- stencil_coef: float32 [2, 9, 128], replicated, may hold values from -4 to 4
- norm_gain: float32 [2, 128], replicated, may hold values from 0.25 to 1.75
- biases: float32 [2, 4, 128], replicated, may hold values from -3 to 3
- weights: bfloat16 [2, 896, 128], P(None, ('lat', 'lon')), may hold values from -0.5 to 0.5
Outputs:
- refined: bfloat16 [1024, 2048, 128], P('lat', 'lon')
All inputs are finite; a program needn't handle non-finite values.
Results may differ from a plain program's by a relative error of at most 0.0069.
Values may be sent and summed in bfloat16 or wider, within the bound.
A program may use at most 128 MiB of HBM per device.

v0:
```python
import jax
import jax.numpy as jnp
from jax import lax
from jax.sharding import PartitionSpec as P

KMAT = 7
ITERS = 2


EPSILON = 1e-05


def extended(cells, sides, width, closed):
    for axis, dim in sides:
        count = lax.axis_size(axis)
        ends = count if closed else count - 1
        head = lax.slice_in_dim(cells, 0, width, axis=dim)
        tail = lax.slice_in_dim(cells, cells.shape[dim] - width, cells.shape[dim], axis=dim)
        cells = jnp.concatenate(
            [
                lax.ppermute(tail, axis, [(i, (i + 1) % count) for i in range(ends)]),
                cells,
                lax.ppermute(head, axis, [((i + 1) % count, i) for i in range(ends)]),
            ],
            axis=dim,
        )
    return cells


def passed_along(block, axis, distance):
    devices = range(lax.axis_size(axis))
    route = [((i - distance) % len(devices), i) for i in devices]
    return lax.ppermute(block, axis, route)


def grid_update(padded_rows, metric_rows, state_rows, coef, gain, bias, mats):
    row_count = state_rows.shape[0]
    col_count = state_rows.shape[1]
    channels = state_rows.shape[2]
    summed = jnp.zeros(state_rows.shape, jnp.float32)
    for lat_step in range(3):
        for lon_step in range(3):
            direction = 3 * lat_step + lon_step
            view = padded_rows[
                lat_step : lat_step + row_count, lon_step : lon_step + col_count
            ].astype(jnp.float32)
            summed = summed + metric_rows[direction][:, :, None] * coef[direction] * view
    scale = lax.rsqrt(jnp.mean(summed * summed, axis=-1, keepdims=True) + EPSILON)
    normed = (summed * scale * gain).astype(jnp.bfloat16).reshape(-1, channels)
    hidden = state_rows.reshape(-1, channels)
    message = (jnp.dot(normed, mats[0], preferred_element_type=jnp.float32) + bias[0]).astype(
        jnp.bfloat16
    )
    update = jax.nn.sigmoid(
        jnp.dot(message, mats[1], preferred_element_type=jnp.float32)
        + jnp.dot(hidden, mats[4], preferred_element_type=jnp.float32)
        + bias[1]
    )
    reset = jax.nn.sigmoid(
        jnp.dot(message, mats[2], preferred_element_type=jnp.float32)
        + jnp.dot(hidden, mats[5], preferred_element_type=jnp.float32)
        + bias[2]
    )
    candidate = jnp.tanh(
        jnp.dot(message, mats[3], preferred_element_type=jnp.float32)
        + bias[3]
        + reset * jnp.dot(hidden, mats[6], preferred_element_type=jnp.float32)
    )
    result = (1.0 - update) * candidate + update * hidden.astype(jnp.float32)
    return result.astype(jnp.bfloat16).reshape(state_rows.shape)


def place_poles(tall, mirrored, band_index, band_count):
    north = jnp.where(band_index == 0, mirrored[0], tall[0])
    south = jnp.where(band_index == band_count - 1, mirrored[1], tall[-1])
    return jnp.concatenate([north[None], tall[1:-1], south[None]], axis=0)


def pad_tile(current, band_index, band_count, half_cycle):
    widened = extended(current, (("lon", 1),), 1, True)
    tall = extended(widened, (("lat", 0),), 1, False)
    mirrored = passed_along(jnp.stack([widened[0], widened[-1]]), "lon", half_cycle)
    return place_poles(tall, mirrored, band_index, band_count)


def on_device(state, edge_metric, stencil_coef, norm_gain, biases, weights):
    gathered = lax.all_gather(weights, ("lat", "lon"), axis=1, tiled=True)
    band_index = lax.axis_index("lat")
    band_count = lax.axis_size("lat")
    half_cycle = lax.axis_size("lon") // 2
    channels = state.shape[2]
    current = state
    for iteration in range(ITERS):
        padded = pad_tile(current, band_index, band_count, half_cycle)
        mats = gathered[iteration].reshape(KMAT, channels, channels)
        current = grid_update(
            padded,
            edge_metric,
            current,
            stencil_coef[iteration],
            norm_gain[iteration],
            biases[iteration],
            mats,
        )
    return current


def solution(mesh):
    in_specs = (
        P("lat", "lon", None),
        P(None, "lat", "lon"),
        P(),
        P(),
        P(),
        P(None, ("lat", "lon"), None),
    )
    out_specs = P("lat", "lon", None)
    return jax.shard_map(
        on_device, mesh=mesh, in_specs=in_specs, out_specs=out_specs, check_vma=False
    )
```

profile of v0, /device:TPU:1, one launch (start us, length us, event | category | flops | bytes accessed | tf_op | source)
XLA Modules:
  0.0 344.8 jit_solution(6598155244749161238)
XLA Ops:
  0.0 1.1 fusion.37
  1.1 2.7 collective-permute-start
  3.8 0.0 collective-permute-start.1
  3.8 1.5 slice_bitcast_fusion.36
  5.3 1.1 slice_bitcast_fusion.8
  6.4 180.8 %all_gather.3 = bf16[2,896,128]{2,0,1:T(2,128)(2,1)S(1)} all-gather(bf16[2,7,128]{2,0,1:T(2,128)(2,1)} %param.11), channel_id=1, replica_groups=mesh['lat'=8,'lon'=16] {'lat','lon'}, dimensions={1}, use_global_device_ids=true | all-gather | bytes 462336 | tf_op jit(solution)/shard_map/all_gather | solution.py:87
  187.2 1.5 fusion.38
  188.7 1.5 slice_bitcast_fusion.11
  190.1 0.0 collective-permute-done
  190.1 0.8 pad_maximum_fusion.11
  190.9 1.3 collective-permute-start.3
  192.2 0.6 pad_maximum_fusion.6
  192.9 1.3 collective-permute-start.4
  194.2 0.3 collective-permute-start.2
  194.5 0.8 slice_bitcast_fusion.13
  195.2 2.4 collective-permute-done.4
  197.7 2.2 collective-permute-done.2
  199.8 0.8 slice_select_fusion.3
  200.7 9.6 %maximum_maximum_fusion = (bf16[129,130,128]{2,1,0:T(8,128)(2,1)S(1)}, bf16[129,130,128]{2,1,0:T(8,128)(2,1)S(1)}) fusion(bf16[128,1,128]{2,1,0:T(2,128)(2,1)S(1)} %collective-permute-done.1, bf16[128,128,128]{2,1,0:T(8,128)(2,1)} %param.6, bf16[128,1,128]{2,1,0:T(2,128)(2,1)S(1)} %collective-permute-done, bf16[1,130,128]{2,1,0:T(8,128)(2,1)S(1)} %get-tuple-element.46, ...), kind=kLoop, calls=%fused_computation.48 | loop fusion | flops 34344960 | bytes 12912640 | tf_op jit(solution)/shard_map/concatenate | solution.py:76
  210.2 24.2 %multiply_reduce_fusion.1 = (f32[128,128]{1,0:T(8,128)S(1)}, f32[128,128,128]{2,1,0:T(8,128)S(1)}) fusion(bf16[129,130,128]{2,1,0:T(8,128)(2,1)S(1)} %get-tuple-element.14, f32[128]{0:T(128)} %get-tuple-element.55, f32[128,128]{1,0:T(8,128)S(1)} %get-tuple-element.28, f32[128]{0:T(128)} %get-tuple-element.56, f32[128,128]{1,0:T(8,128)S(1)} %get-tuple-element.29, ...), kind=kLoop, calls=%fused_computation.46 | loop fusion | flops 90161152 | bytes 38474240 | tf_op jit(solution)/shard_map/reduce_sum | solution.py:48
  234.5 4.7 %multiply_convert_fusion.1 = bf16[128,128,128]{2,1,0:T(8,128)(2,1)S(1)} fusion(f32[128,128,128]{2,1,0:T(8,128)S(1)} %get-tuple-element.8, f32[128]{0:T(128)S(1)} %get-tuple-element.75, f32[128,128]{1,0:T(8,128)S(1)} %add_rsqrt_fusion.1), kind=kLoop, calls=%fused_computation.45 | loop fusion | flops 6291456 | bytes 12648960 | tf_op jit(solution)/shard_map/convert_element_type | solution.py:49
  239.2 1.2 fusion.26
  240.5 1.2 fusion.35
  241.7 1.2 fusion.34
  243.0 4.5 %convolution_add_fusion.5 = f32[16384,128]{1,0:T(8,128)} fusion(bf16[16384,128]{1,0:T(8,128)(2,1)S(1)} %fusion.26, f32[128]{0:T(128)S(1)} %get-tuple-element.69, bf16[1,128,128]{2,0,1:T(2,128)(2,1)S(1)} %get-tuple-element.40), kind=kOutput, calls=%fused_computation.25 | convolution fusion | flops 538968064 | bytes 12616192 | tf_op jit(solution)/shard_map/dot_general | solution.py:65
  247.5 4.6 %fusion.28 = f32[16384,128]{1,0:T(8,128)} fusion(f32[16384,128]{1,0:T(8,128)S(1)} %fusion.35, bf16[16384,128]{1,0:T(8,128)(2,1)S(1)} %bitcast.139, f32[128]{0:T(128)S(1)} %copy-done.17, bf16[1,128,128]{2,0,1:T(2,128)(2,1)S(1)} %copy-done.4), kind=kOutput, calls=%fused_computation.38 | convolution fusion | flops 547356672 | bytes 21004800 | tf_op jit(solution)/shard_map/dot_general | solution.py:56
  252.1 4.6 %fusion.29 = f32[16384,128]{1,0:T(8,128)} fusion(f32[16384,128]{1,0:T(8,128)S(1)} %fusion.34, bf16[16384,128]{1,0:T(8,128)(2,1)S(1)} %bitcast.140, f32[128]{0:T(128)S(1)} %copy-done.16, bf16[1,128,128]{2,0,1:T(2,128)(2,1)S(1)} %copy-done.3), kind=kOutput, calls=%fused_computation.39 | convolution fusion | flops 547356672 | bytes 21004800 | tf_op jit(solution)/shard_map/dot_general | solution.py:61
  256.7 9.8 %fusion.25 = bf16[16384,128]{1,0:T(8,128)(2,1)S(1)} fusion(f32[16384,128]{1,0:T(8,128)} %convolution_add_fusion.5, f32[16384,128]{1,0:T(8,128)} %fusion.29, bf16[16384,128]{1,0:T(8,128)(2,1)S(1)} %bitcast.141, f32[16384,128]{1,0:T(8,128)} %fusion.28, bf16[1,128,128]{2,0,1:T(2,128)(2,1)S(1)} %get-tuple-element.37), kind=kOutput, calls=%fused_computation.35 | convolution fusion | flops 553648128 | bytes 33587200 | tf_op jit(solution)/shard_map/dot_general | solution.py:67
  266.4 0.1 fusion.36
  266.5 0.1 collective-permute-start.5
  266.7 1.1 collective-permute-start.6
  267.8 0.6 collective-permute-done.5
  268.4 2.1 collective-permute-done.6
  270.5 0.4 collective-permute-start.7
  270.9 4.2 %collective-permute-start.8 = (bf16[1,130,128]{2,1,0:T(8,128)(2,1)S(1)}, bf16[1,130,128]{2,1,0:T(8,128)(2,1)S(1)}, u32[]{:S(2)}, u32[]{:S(2)}) collective-permute-start(bf16[1,130,128]{2,1,0:T(8,128)(2,1)S(1)} %get-tuple-element.11), channel_id=1, source_target_pairs={{0,16},{16,32},{32,48},{48,64},{64,80},{80,96},{96,112},{1,17},{17... | collective-permute-start | bytes 99848 | tf_op jit(solution)/shard_map/ppermute | solution.py:21
  275.1 1.3 collective-permute-start.9
  276.4 4.0 %collective-permute-done.9 = bf16[1,130,128]{2,1,0:T(8,128)(2,1)S(1)} collective-permute-done((bf16[1,130,128]{2,1,0:T(8,128)(2,1)S(1)}, bf16[1,130,128]{2,1,0:T(8,128)(2,1)S(1)}, u32[]{:S(2)}, u32[]{:S(2)}) %collective-permute-start.9) | collective-permute-done | bytes 33312 | tf_op jit(solution)/shard_map/ppermute | solution.py:23
  280.4 0.0 collective-permute-done.7
  280.5 6.8 %maximum_maximum_fusion.1 = (bf16[129,130,128]{2,1,0:T(8,128)(2,1)S(1)}, bf16[129,130,128]{2,1,0:T(8,128)(2,1)S(1)}) fusion(bf16[128,1,128]{2,1,0:T(2,128)(2,1)S(1)} %collective-permute-done.6, bf16[128,128,128]{2,1,0:T(8,128)(2,1)S(1)} %bitcast.137, bf16[128,1,128]{2,1,0:T(2,128)(2,1)S(1)} %collective-permute-done.5, ...), kind=kLoop, calls=%fused_computation.50 | loop fusion | flops 34344960 | bytes 12912640 | tf_op jit(solution)/shard_map/concatenate | solution.py:76
  287.4 23.4 %multiply_reduce_fusion = (f32[128,128]{1,0:T(8,128)S(1)}, f32[128,128,128]{2,1,0:T(8,128)S(1)}) fusion(bf16[129,130,128]{2,1,0:T(8,128)(2,1)S(1)} %get-tuple-element.10, f32[128]{0:T(128)S(1)} %copy-done.12, f32[128,128]{1,0:T(8,128)S(1)} %get-tuple-element.28, f32[128]{0:T(128)S(1)} %copy-done.13, f32[128,128]{1,0:T(8,128)S(1)} %get-tuple-element.29, ...), kind=kLoop, calls=%fused_computation.43 | loop fusion | flops 90161152 | bytes 38474240 | tf_op jit(solution)/shard_map/reduce_sum | solution.py:48
  310.8 4.7 %multiply_convert_fusion = bf16[128,128,128]{2,1,0:T(8,128)(2,1)S(1)} fusion(f32[128,128,128]{2,1,0:T(8,128)S(1)} %get-tuple-element.6, f32[128]{0:T(128)S(1)} %get-tuple-element.74, f32[128,128]{1,0:T(8,128)S(1)} %add_rsqrt_fusion), kind=kLoop, calls=%fused_computation.42 | loop fusion | flops 6291456 | bytes 12648960 | tf_op jit(solution)/shard_map/convert_element_type | solution.py:49
  315.6 1.2 fusion.27
  316.8 1.2 fusion.33
  318.0 1.2 fusion.32
  319.3 4.5 %convolution_add_fusion.1 = f32[16384,128]{1,0:T(8,128)} fusion(bf16[16384,128]{1,0:T(8,128)(2,1)S(1)} %fusion.27, f32[128]{0:T(128)S(1)} %get-tuple-element.73, bf16[1,128,128]{2,0,1:T(2,128)(2,1)S(1)} %get-tuple-element.33), kind=kOutput, calls=%fused_computation.9 | convolution fusion | flops 538968064 | bytes 12616192 | tf_op jit(solution)/shard_map/dot_general | solution.py:65
  323.8 4.5 %fusion.30 = f32[16384,128]{1,0:T(8,128)} fusion(f32[16384,128]{1,0:T(8,128)S(1)} %fusion.33, bf16[16384,128]{1,0:T(8,128)(2,1)S(1)} %fusion.25, f32[128]{0:T(128)S(1)} %copy-done.15, bf16[1,128,128]{2,0,1:T(2,128)(2,1)S(1)} %copy-done.2), kind=kOutput, calls=%fused_computation.40 | convolution fusion | flops 547356672 | bytes 21004800 | tf_op jit(solution)/shard_map/dot_general | solution.py:56
  328.4 4.6 %fusion.31 = f32[16384,128]{1,0:T(8,128)} fusion(f32[16384,128]{1,0:T(8,128)S(1)} %fusion.32, bf16[16384,128]{1,0:T(8,128)(2,1)S(1)} %fusion.25, f32[128]{0:T(128)S(1)} %copy-done.14, bf16[1,128,128]{2,0,1:T(2,128)(2,1)S(1)} %copy-done.1), kind=kOutput, calls=%fused_computation.41 | convolution fusion | flops 547356672 | bytes 21004800 | tf_op jit(solution)/shard_map/dot_general | solution.py:61
  333.0 11.8 %fusion.24 = bf16[16384,128]{1,0:T(8,128)(2,1)} fusion(f32[16384,128]{1,0:T(8,128)} %convolution_add_fusion.1, f32[16384,128]{1,0:T(8,128)} %fusion.31, bf16[16384,128]{1,0:T(8,128)(2,1)S(1)} %fusion.25, f32[16384,128]{1,0:T(8,128)} %fusion.30, bf16[1,128,128]{2,0,1:T(2,128)(2,1)S(1)} %get-tuple-element.30), kind=kOutput, calls=%fused_computation.34 | convolution fusion | flops 553648128 | bytes 33587200 | tf_op jit(solution)/shard_map/dot_general | solution.py:67
  (44 shorter events, 0.2 us)
Async XLA Ops:
  1.1 189.0 %collective-permute-start = (bf16[128,1,128]{2,1,0:T(2,128)(2,1)S(1)}, bf16[128,1,128]{2,1,0:T(2,128)(2,1)S(1)}, u32[]{:S(2)}, u32[]{:S(2)}) collective-permute-start(bf16[128,1,128]{2,1,0:T(2,128)(2,1)S(1)} %get-tuple-element.19), channel_id=1, source_target_pairs={{0,1},{1,2},{2,3},{3,4},{4,5},{5,6},{6,7},{7,8},{8,9},{9,10},{10,1... | collective-permute-start | bytes 98312 | tf_op jit(solution)/shard_map/ppermute | solution.py:21
  3.8 186.3 %collective-permute-start.1 = (bf16[128,1,128]{2,1,0:T(2,128)(2,1)S(1)}, bf16[128,1,128]{2,1,0:T(2,128)(2,1)S(1)}, u32[]{:S(2)}, u32[]{:S(2)}) collective-permute-start(bf16[128,1,128]{2,1,0:T(2,128)(2,1)S(1)} %get-tuple-element.20), channel_id=1, source_target_pairs={{1,0},{2,1},{3,2},{4,3},{5,4},{6,5},{7,6},{8,7},{9,8},{10,9},{11,1... | collective-permute-start | bytes 98312 | tf_op jit(solution)/shard_map/ppermute | solution.py:23
  190.9 4.3 %collective-permute-start.3 = (bf16[1,130,128]{2,1,0:T(8,128)(2,1)S(1)}, bf16[1,130,128]{2,1,0:T(8,128)(2,1)S(1)}, u32[]{:S(2)}, u32[]{:S(2)}) collective-permute-start(bf16[1,130,128]{2,1,0:T(8,128)(2,1)S(1)} %get-tuple-element.15), channel_id=1, source_target_pairs={{0,16},{16,32},{32,48},{48,64},{64,80},{80,96},{96,112},{1,17},{17... | collective-permute-start | bytes 99848 | tf_op jit(solution)/shard_map/ppermute | solution.py:21
  192.9 4.8 %collective-permute-start.4 = (bf16[1,130,128]{2,1,0:T(8,128)(2,1)S(1)}, bf16[1,130,128]{2,1,0:T(8,128)(2,1)}, u32[]{:S(2)}, u32[]{:S(2)}) collective-permute-start(bf16[1,130,128]{2,1,0:T(8,128)(2,1)S(1)} %get-tuple-element.16), channel_id=1, source_target_pairs={{16,0},{32,16},{48,32},{64,48},{80,64},{96,80},{112,96},{17,1},{33... | collective-permute-start | bytes 99848 | tf_op jit(solution)/shard_map/ppermute | solution.py:23
  194.2 5.7 %collective-permute-start.2 = (bf16[2,130,128]{2,1,0:T(8,128)(2,1)}, bf16[2,130,128]{2,1,0:T(8,128)(2,1)}, u32[]{:S(2)}, u32[]{:S(2)}) collective-permute-start(bf16[2,130,128]{2,1,0:T(8,128)(2,1)} %pad_maximum_fusion.6), channel_id=1, source_target_pairs={{8,0},{9,1},{10,2},{11,3},{12,4},{13,5},{14,6},{15,7},{0,8},{1,9},... | collective-permute-start | bytes 199688 | tf_op jit(solution)/shard_map/ppermute | solution.py:33
  195.2 15.0 %copy-start = (bf16[128,128,128]{2,1,0:T(8,128)(2,1)S(1)}, bf16[128,128,128]{2,1,0:T(8,128)(2,1)}, u32[]{:S(2)}) copy-start(bf16[128,128,128]{2,1,0:T(8,128)(2,1)} %param.6) | copy-start | bytes 12582916
  243.0 4.5 %copy-start.4 = (bf16[1,128,128]{2,0,1:T(2,128)(2,1)S(1)}, bf16[1,128,128]{2,0,1:T(2,128)(2,1)}, u32[]{:S(2)}) copy-start(bf16[1,128,128]{2,0,1:T(2,128)(2,1)} %get-tuple-element.41) | copy-start | bytes 98308
  243.0 4.5 %copy-start.17 = (f32[128]{0:T(128)S(1)}, f32[128]{0:T(128)}, u32[]{:S(2)}) copy-start(f32[128]{0:T(128)} %get-tuple-element.70) | copy-start | bytes 1540
  247.5 4.6 %copy-start.3 = (bf16[1,128,128]{2,0,1:T(2,128)(2,1)S(1)}, bf16[1,128,128]{2,0,1:T(2,128)(2,1)}, u32[]{:S(2)}) copy-start(bf16[1,128,128]{2,0,1:T(2,128)(2,1)} %get-tuple-element.38) | copy-start | bytes 98308
  247.5 4.6 %copy-start.16 = (f32[128]{0:T(128)S(1)}, f32[128]{0:T(128)}, u32[]{:S(2)}) copy-start(f32[128]{0:T(128)} %get-tuple-element.68) | copy-start | bytes 1540
  266.5 1.8 collective-permute-start.5
  266.6 20.7 %copy-start.5 = (f32[128]{0:T(128)S(1)}, f32[128]{0:T(128)}, u32[]{:S(2)}) copy-start(f32[128]{0:T(128)} %get-tuple-element.48) | copy-start | bytes 1540
  266.6 20.7 %copy-start.6 = (f32[128]{0:T(128)S(1)}, f32[128]{0:T(128)}, u32[]{:S(2)}) copy-start(f32[128]{0:T(128)} %get-tuple-element.49) | copy-start | bytes 1540
  266.6 20.7 %copy-start.7 = (f32[128]{0:T(128)S(1)}, f32[128]{0:T(128)}, u32[]{:S(2)}) copy-start(f32[128]{0:T(128)} %get-tuple-element.50) | copy-start | bytes 1540
  266.7 20.7 %copy-start.8 = (f32[128]{0:T(128)S(1)}, f32[128]{0:T(128)}, u32[]{:S(2)}) copy-start(f32[128]{0:T(128)} %get-tuple-element.51) | copy-start | bytes 1540
  266.7 20.7 %copy-start.9 = (f32[128]{0:T(128)S(1)}, f32[128]{0:T(128)}, u32[]{:S(2)}) copy-start(f32[128]{0:T(128)} %get-tuple-element.52) | copy-start | bytes 1540
  266.7 20.7 %copy-start.10 = (f32[128]{0:T(128)S(1)}, f32[128]{0:T(128)}, u32[]{:S(2)}) copy-start(f32[128]{0:T(128)} %get-tuple-element.53) | copy-start | bytes 1540
  266.7 20.7 %copy-start.11 = (f32[128]{0:T(128)S(1)}, f32[128]{0:T(128)}, u32[]{:S(2)}) copy-start(f32[128]{0:T(128)} %get-tuple-element.54) | copy-start | bytes 1540
  266.7 20.7 %copy-start.12 = (f32[128]{0:T(128)S(1)}, f32[128]{0:T(128)}, u32[]{:S(2)}) copy-start(f32[128]{0:T(128)} %get-tuple-element.64) | copy-start | bytes 1540
  266.7 20.7 %copy-start.13 = (f32[128]{0:T(128)S(1)}, f32[128]{0:T(128)}, u32[]{:S(2)}) copy-start(f32[128]{0:T(128)} %get-tuple-element.65) | copy-start | bytes 1540
  266.7 3.8 %collective-permute-start.6 = (bf16[128,1,128]{2,1,0:T(2,128)(2,1)S(1)}, bf16[128,1,128]{2,1,0:T(2,128)(2,1)S(1)}, u32[]{:S(2)}, u32[]{:S(2)}) collective-permute-start(bf16[128,1,128]{2,1,0:T(2,128)(2,1)S(1)} %get-tuple-element.18), channel_id=1, source_target_pairs={{1,0},{2,1},{3,2},{4,3},{5,4},{6,5},{7,6},{8,7},{9,8},{10,9},{11,1... | collective-permute-start | bytes 98312 | tf_op jit(solution)/shard_map/ppermute | solution.py:23
  270.5 9.9 %collective-permute-start.7 = (bf16[2,130,128]{2,1,0:T(8,128)(2,1)S(1)}, bf16[2,130,128]{2,1,0:T(8,128)(2,1)S(1)}, u32[]{:S(2)}, u32[]{:S(2)}) collective-permute-start(bf16[2,130,128]{2,1,0:T(8,128)(2,1)S(1)} %pad_maximum_fusion.7), channel_id=1, source_target_pairs={{8,0},{9,1},{10,2},{11,3},{12,4},{13,5},{14,6},{15,7},{0,8},{1,9},... | collective-permute-start | bytes 199688 | tf_op jit(solution)/shard_map/ppermute | solution.py:33
  270.9 5.5 %collective-permute-start.8 = (bf16[1,130,128]{2,1,0:T(8,128)(2,1)S(1)}, bf16[1,130,128]{2,1,0:T(8,128)(2,1)S(1)}, u32[]{:S(2)}, u32[]{:S(2)}) collective-permute-start(bf16[1,130,128]{2,1,0:T(8,128)(2,1)S(1)} %get-tuple-element.11), channel_id=1, source_target_pairs={{0,16},{16,32},{32,48},{48,64},{64,80},{80,96},{96,112},{1,17},{17... | collective-permute-start | bytes 99848 | tf_op jit(solution)/shard_map/ppermute | solution.py:21
  275.1 5.3 %collective-permute-start.9 = (bf16[1,130,128]{2,1,0:T(8,128)(2,1)S(1)}, bf16[1,130,128]{2,1,0:T(8,128)(2,1)S(1)}, u32[]{:S(2)}, u32[]{:S(2)}) collective-permute-start(bf16[1,130,128]{2,1,0:T(8,128)(2,1)S(1)} %get-tuple-element.12), channel_id=1, source_target_pairs={{16,0},{32,16},{48,32},{64,48},{80,64},{96,80},{112,96},{17,1},{33... | collective-permute-start | bytes 99848 | tf_op jit(solution)/shard_map/ppermute | solution.py:23
  319.3 4.5 %copy-start.2 = (bf16[1,128,128]{2,0,1:T(2,128)(2,1)S(1)}, bf16[1,128,128]{2,0,1:T(2,128)(2,1)}, u32[]{:S(2)}) copy-start(bf16[1,128,128]{2,0,1:T(2,128)(2,1)} %get-tuple-element.34) | copy-start | bytes 98308
  319.3 4.5 %copy-start.15 = (f32[128]{0:T(128)S(1)}, f32[128]{0:T(128)}, u32[]{:S(2)}) copy-start(f32[128]{0:T(128)} %get-tuple-element.66) | copy-start | bytes 1540
  323.8 4.6 %copy-start.1 = (bf16[1,128,128]{2,0,1:T(2,128)(2,1)S(1)}, bf16[1,128,128]{2,0,1:T(2,128)(2,1)}, u32[]{:S(2)}) copy-start(bf16[1,128,128]{2,0,1:T(2,128)(2,1)} %get-tuple-element.31) | copy-start | bytes 98308
  323.8 4.6 %copy-start.14 = (f32[128]{0:T(128)S(1)}, f32[128]{0:T(128)}, u32[]{:S(2)}) copy-start(f32[128]{0:T(128)} %get-tuple-element.72) | copy-start | bytes 1540
where the time goes:
time: 351 us; the launch traced here: 345 us
  blocking collectives  181 us (52%)
  other arithmetic  75.8 us (22%)
  matrix products  56.3 us (16%)
  starting transfers between devices  12.5 us (4%)
  waiting for transfers between devices  11.3 us (3%)
  local copies, waits for them, and re-layouts  7.64 us (2%)
    all_gather x1, blocking collectives, on_device(): gathered = lax.all_gather(weights, ('lat', 'lon'), axis=1, tiled=True)  181 us
    reduce_sum x2, other arithmetic, grid_update(): jnp.mean(summed * summed, axis=-1, keepdims=True) + EPSILON  47.6 us
    dot_general x2, matrix products, grid_update(): jnp.dot(hidden, mats[6], preferred_element_type=jnp.float32)  21.6 us
    concatenate x2, other arithmetic, place_poles(): return jnp.concatenate([north[None], tall[1:-1], south[None]], axis=0)  16.4 us
    convert_element_type x2, other arithmetic, grid_update(): normed = (summed * scale * gain).astype(jnp.bfloat16).reshape(-1, channels)  9.45 us
    dot_general x2, matrix products, grid_update(): jnp.dot(hidden, mats[5], preferred_element_type=jnp.float32)  9.18 us
    dot_general x2, matrix products, grid_update(): jnp.dot(hidden, mats[4], preferred_element_type=jnp.float32)  9.11 us
    dot_general x2, matrix products, grid_update(): jnp.dot(message, mats[3], preferred_element_type=jnp.float32) + bias[3]  9.03 us
  transfers between devices with their start and end apart: 10, of which 5 were waited for; matrix products, arithmetic and copies ran while one was open for 2% of the time, Pallas kernels for 0%

commit v1 on v0

v1 whole, which is shorter than its diff:
```python
import jax
import jax.numpy as jnp
from jax import lax
from jax.experimental import pallas as pl
from jax.experimental.pallas import tpu as pltpu
from jax.sharding import PartitionSpec as P

F32, BF16 = jnp.float32, jnp.bfloat16
EPSILON = 1e-05
ROWS = 128
RI = 4
RG = 8
MESH = pl.DeviceIdType.MESH


def lane_iota(shape):
    return lax.broadcasted_iota(jnp.int32, shape, len(shape) - 1)


def stencil_block(i0, xl, xc, xr, met, coef, t, agg, nrm):
    ss = [None] * RI
    for c0 in range(0, 16, 2):
        m = {}
        for cb in range(c0, c0 + 2):
            cs = slice(8 * cb, 8 * cb + 8)
            cf = [coef[t, d, cs, :] for d in range(9)]
            acc = [None] * RI
            for p in range(RI + 2):
                xs = [ref[i0 + p, cs, :] for ref in (xl, xc, xr)]
                for a in range(3):
                    r = p - a
                    if 0 <= r < RI:
                        for b in range(3):
                            d = 3 * a + b
                            if (d, r) not in m:
                                m[d, r] = jnp.broadcast_to(met[d, pl.ds(i0 + r, 1), :], (8, 128))
                            term = (m[d, r] * cf[d]) * xs[b]
                            acc[r] = term if acc[r] is None else acc[r] + term
            for r in range(RI):
                agg[r, cs, :] = acc[r]
                sq = acc[r] * acc[r]
                ss[r] = sq if ss[r] is None else ss[r] + sq
    for r in range(RI):
        scale = lax.rsqrt(jnp.sum(ss[r], axis=0, keepdims=True) * (1.0 / 128) + EPSILON)
        nrm[i0 + r] = (agg[r] * scale).astype(BF16)


def gate_block(i0, nrm, xc, wt, bias, t, emit):
    h = [xc[i0 + 1 + r] for r in range(RG)]
    z = jnp.concatenate(
        [
            jnp.concatenate([nrm[i0 + r] for r in range(RG)], axis=1),
            jnp.concatenate([v.astype(BF16) for v in h], axis=1),
        ],
        axis=0,
    )
    y = jnp.dot(wt[t], z, preferred_element_type=F32)
    for g in range(8):
        cs = slice(16 * g, 16 * g + 16)
        b0, b1, b2 = (bias[t, k, cs, :] for k in range(3))
        outs = []
        for r in range(RG):
            ls = slice(128 * r, 128 * r + 128)
            q = y[64 * g + 48 : 64 * g + 64, ls]
            u = jnp.tanh(y[64 * g : 64 * g + 16, ls] + b0)
            v = jnp.tanh(y[64 * g + 16 : 64 * g + 32, ls] + b1)
            c = jnp.tanh(y[64 * g + 32 : 64 * g + 48, ls] + b2 + v * q)
            hh = h[r][cs]
            outs.append((0.5 * ((hh + c) + u * (hh - c))).astype(BF16))
        emit(cs, outs)


def slot_owner(s):
    core, y, z, x = s // 64, (s // 16) % 4, (s // 4) % 4, s % 4
    return (y * 2 + z % 2) * 16 + (z // 2) * 8 + x * 2 + core


def prepare_weights(t, wg, w32, gain, bvec, wt, bias):
    for s in range(128):
        w32[pl.ds(7 * slot_owner(s), 7), :] = wg[s, t].astype(F32)
    mt = [w32[128 * k : 128 * k + 128, :].T.astype(BF16) for k in range(7)]
    grow = gain[t : t + 1, :]
    column = lambda k: jnp.broadcast_to(bvec[t, k : k + 1, :], (128, 128)).T
    b0 = column(0)
    hi = b0.astype(BF16)
    lo = (b0 - hi.astype(F32)).astype(BF16)
    split = jnp.concatenate([hi, lo], axis=0)
    left = []
    for k in (1, 2, 3):
        half = 1.0 if k == 3 else 0.5
        fold = jnp.dot(mt[k], mt[0], preferred_element_type=F32)
        left.append((fold * grow * half).astype(BF16))
        extra = jnp.dot(
            jnp.concatenate([mt[k], mt[k]], axis=1), split, preferred_element_type=F32
        )
        bias[t, k - 1] = (extra + column(k)) * half
    right = [(mt[k].astype(F32) * 0.5).astype(BF16) for k in (4, 5, 6, 6)]
    left.append(jnp.zeros((128, 128), BF16))
    for g in range(8):
        for k in range(4):
            rows = slice(64 * g + 16 * k, 64 * g + 16 * k + 16)
            wt[t, rows, :128] = left[k][16 * g : 16 * g + 16]
            wt[t, rows, 128:] = right[k][16 * g : 16 * g + 16]


def kernel(
    state, met_h, coef_h, gain_h, bias_h, w_h, out,
    xnat, xl, xc, xr, nrm, stage, met, coef_v, gain, bvec, coef, agg, wg, w32, wt, bias,
    gnat, gnat_r, gacc, gsend, grecv, gw, ge, rsend, rrecv,
    in_sem, w_sem, ag_send, ag_recv, gn_send, gn_recv, gb_send, gb_recv, rr_send, rr_recv, out_sem,
):
    lat, lon = lax.axis_index("lat"), lax.axis_index("lon")
    y, z_lo = lat // 2, lat % 2
    z_hi, x, core = lon // 8, (lon // 2) % 4, lon % 2
    z = z_hi * 2 + z_lo

    def place(py, pz, px, pcore):
        return (py * 2 + pz % 2, (pz // 2) * 8 + px * 2 + pcore)

    def slot_of(py, pz, px, pcore):
        return pcore * 64 + py * 16 + pz * 4 + px

    east, west = (lat, (lon + 1) % 16), (lat, (lon + 15) % 16)
    top, bottom = lat == 0, lat == 7
    mirror = (lon + 8) % 16
    north = (jnp.where(top, lat, lat - 1), jnp.where(top, mirror, lon))
    south = (jnp.where(bottom, lat, lat + 1), jnp.where(bottom, mirror, lon))
    north_slot = jnp.where(top, 0, 1)
    south_slot = jnp.where(bottom, 1, 0)

    quarter = ROWS // 4
    loads = [
        pltpu.make_async_copy(
            state.at[pl.ds(quarter * q, quarter)], xnat.at[pl.ds(quarter * q, quarter)], in_sem.at[q]
        )
        for q in range(4)
    ]
    own = slot_of(y, z, x, core)
    load_w = pltpu.make_async_copy(w_h, wg.at[own], w_sem)
    load_w.start()
    for copy in loads:
        copy.start()
    smalls = [
        pltpu.make_async_copy(src, dst, in_sem.at[4 + k])
        for k, (src, dst) in enumerate(
            ((met_h, met), (coef_h, coef_v), (gain_h, gain), (bias_h, bvec))
        )
    ]
    for copy in smalls:
        copy.start()

    barrier = pltpu.get_barrier_semaphore()
    partners = [east, west, north, south, place(y, z, x, 1 - core)]
    for k in (1, 2, 3):
        partners += [
            place(y, z, (x + k) % 4, core),
            place(y, (z + k) % 4, x, core),
            place((y + k) % 4, z, x, core),
        ]
    for partner in partners:
        pl.semaphore_signal(barrier, inc=1, device_id=partner, device_id_type=MESH)
    pl.semaphore_wait(barrier, len(partners))

    def hop(stage_no, k, count, first, target):
        block = wg.at[pl.ds(first, count)]
        return pltpu.make_async_remote_copy(
            src_ref=block, dst_ref=block,
            send_sem=ag_send.at[stage_no, k], recv_sem=ag_recv.at[stage_no, k],
            device_id=target, device_id_type=MESH,
        )

    def stage_copies(stage_no):
        sends, receives = [], []
        for k in (1, 2, 3):
            if stage_no == 0:
                count, first = 1, slot_of(y, z, x, core)
                target, source = place(y, z, (x + k) % 4, core), (x + 4 - k) % 4
                arriving = slot_of(y, z, source, core)
            elif stage_no == 1:
                count, first = 4, slot_of(y, z, 0, core)
                target, source = place(y, (z + k) % 4, x, core), (z + 4 - k) % 4
                arriving = slot_of(y, source, 0, core)
            else:
                count, first = 16, slot_of(y, 0, 0, core)
                target, source = place((y + k) % 4, z, x, core), (y + 4 - k) % 4
                arriving = slot_of(source, 0, 0, core)
            sends.append(hop(stage_no, k - 1, count, first, target))
            receives.append(hop(stage_no, k - 1, count, arriving, target))
        return sends, receives

    def start_all(copies):
        for copy in copies:
            copy.start()

    def wait_stage(copies):
        for send, receive in zip(*copies):
            send.wait_send()
            receive.wait_recv()

    load_w.wait()
    along_x = stage_copies(0)
    start_all(along_x[0])

    for q in range(4):
        loads[q].wait()

        def edges(s, carry, q=q):
            for k in range(8):
                i = quarter * q + s * 8 + k
                gnat[0, pl.ds(i, 1), :] = xnat[i, 0:16, :].astype(F32)[0:1]
                gnat[1, pl.ds(i, 1), :] = xnat[i, 112:128, :].astype(F32)[15:16]
            return carry

        lax.fori_loop(0, quarter // 8, edges, 0)

    def side(src, dst, ssem, rsem, target):
        return pltpu.make_async_remote_copy(
            src_ref=src, dst_ref=dst, send_sem=ssem, recv_sem=rsem,
            device_id=target, device_id_type=MESH,
        )

    first_sides = [
        side(gnat.at[0], gnat_r.at[0], gn_send.at[0], gn_recv.at[0], west),
        side(gnat.at[1], gnat_r.at[1], gn_send.at[1], gn_recv.at[1], east),
    ]
    start_all(first_sides)
    wait_stage(along_x)
    along_z = stage_copies(1)
    start_all(along_z[0])

    def turn(s, carry):
        for k in range(8):
            i = s * 8 + k
            xc[i + 1] = xnat[i].T.astype(F32)
        return carry

    lax.fori_loop(0, ROWS // 16, turn, 0)
    wait_stage(along_z)
    along_y = stage_copies(2)
    start_all(along_y[0])
    lax.fori_loop(ROWS // 16, ROWS // 8, turn, 0)

    for copy in smalls:
        copy.wait()
    for t in range(2):
        for d in range(9):
            coef[t, d] = jnp.broadcast_to(coef_v[t, d : d + 1, :], (128, 128)).T

    for copy in first_sides:
        copy.wait()
    ge[...] = gnat_r[0].T
    gw[...] = pltpu.roll(gnat_r[1].T, 127, 1)
    wait_stage(along_y)
    other = 1 - core
    across = (
        [hop(3, 0, 64, core * 64, place(y, z, x, other))],
        [hop(3, 0, 64, other * 64, place(y, z, x, other))],
    )
    start_all(across[0])

    lane8 = lane_iota((8, 128))

    def build_row(i):
        left_shift, right_shift = (129 - i) % 128, 127 - i
        for cb in range(16):
            cs = slice(8 * cb, 8 * cb + 8)
            v = xc[i + 1, cs, :]
            xl[i + 1, cs, :] = jnp.where(
                lane8 == 0, pltpu.roll(gw[cs, :], left_shift, 1), pltpu.roll(v, 1, 1)
            )
            xr[i + 1, cs, :] = jnp.where(
                lane8 == 127, pltpu.roll(ge[cs, :], right_shift, 1), pltpu.roll(v, 127, 1)
            )

    def stencil_phase(t):
        def early(s, carry):
            build_row(jnp.where(s == 0, 127, s - 1))
            return carry

        lax.fori_loop(0, 10, early, 0)
        for edge, row in ((0, 1), (1, ROWS)):
            for part, ref in enumerate((xl, xc, xr)):
                rsend[t, edge, part] = ref[row].astype(BF16)
        rows = [
            side(rsend.at[t, 0], rrecv.at[t, north_slot], rr_send.at[t, 0], rr_recv.at[t, north_slot], north),
            side(rsend.at[t, 1], rrecv.at[t, south_slot], rr_send.at[t, 1], rr_recv.at[t, south_slot], south),
        ]
        start_all(rows)

        def inner(s, carry):
            i0 = s * RI
            stencil_block(i0, xl, xc, xr, met, coef, t, agg, nrm)
            for k in range(RI):
                build_row(jnp.minimum(i0 + RI + 1 + k, 127))
            return carry

        lax.fori_loop(1, ROWS // RI - 1, inner, 0)
        for copy in rows:
            copy.wait_send()
        for edge, target in ((0, north), (1, south)):
            side(
                rsend.at[t, edge], rrecv.at[t, edge], rr_send.at[t, edge], rr_recv.at[t, edge], target
            ).wait_recv()
        for edge, row in ((0, 0), (1, ROWS + 1)):
            for part, ref in enumerate((xl, xc, xr)):
                ref[row] = rrecv[t, edge, part].astype(F32)

        def outer(s, carry):
            stencil_block(jnp.where(s == 0, 0, ROWS - RI), xl, xc, xr, met, coef, t, agg, nrm)
            return carry

        lax.fori_loop(0, 2, outer, 0)

    stencil_phase(0)

    wait_stage(across)
    for t in range(2):
        prepare_weights(t, wg, w32, gain, bvec, wt, bias)

    lane16 = lane_iota((16, 128))

    def gates_first(s, carry):
        i0 = s * RG

        def emit(cs, outs):
            head, tail = gacc[0, cs, :], gacc[1, cs, :]
            for r in range(RG):
                i = i0 + r
                v = outs[r].astype(F32)
                xc[i + 1, cs, :] = v
                turned = pltpu.roll(v, i, 1)
                head = jnp.where(lane16 == i, turned, head)
                tail = jnp.where(lane16 == (i + 127) % 128, turned, tail)
            gacc[0, cs, :] = head
            gacc[1, cs, :] = tail

        gate_block(i0, nrm, xc, wt, bias, 0, emit)
        return carry

    gacc[...] = jnp.zeros_like(gacc)
    lax.fori_loop(0, ROWS // RG, gates_first, 0)
    gsend[...] = gacc[...].astype(BF16)
    second_sides = [
        side(gsend.at[0], grecv.at[0], gb_send.at[0], gb_recv.at[0], west),
        side(gsend.at[1], grecv.at[1], gb_send.at[1], gb_recv.at[1], east),
    ]
    start_all(second_sides)
    for copy in second_sides:
        copy.wait()
    ge[...] = grecv[0].astype(F32)
    gw[...] = grecv[1].astype(F32)

    stencil_phase(1)

    def gates_second(s, carry):
        i0 = s * RG
        kept = [[] for _ in range(RG)]

        def emit(cs, outs):
            for r in range(RG):
                kept[r].append(outs[r])

        gate_block(i0, nrm, xc, wt, bias, 1, emit)
        for r in range(RG):
            stage[i0 + r] = jnp.concatenate(kept[r], axis=0).T
        pltpu.make_async_copy(
            stage.at[pl.ds(i0, RG)], out.at[pl.ds(i0, RG)], out_sem
        ).start()
        return carry

    lax.fori_loop(0, ROWS // RG, gates_second, 0)
    pltpu.make_async_copy(stage, out, out_sem).wait()


def on_device(state, edge_metric, stencil_coef, norm_gain, biases, weights):
    anywhere = pl.BlockSpec(memory_space=pl.ANY)
    cube = (ROWS, 128, 128)
    tall = (ROWS + 2, 128, 128)
    dma, vmem = pltpu.SemaphoreType.DMA, pltpu.VMEM
    return pl.pallas_call(
        kernel,
        out_shape=jax.ShapeDtypeStruct(cube, BF16),
        in_specs=[anywhere] * 6,
        out_specs=anywhere,
        scratch_shapes=[
            vmem(cube, BF16), vmem(tall, F32), vmem(tall, F32), vmem(tall, F32),
            vmem(cube, BF16), vmem(cube, BF16),
            vmem((9, 128, 128), F32), vmem((2, 9, 128), F32), vmem((2, 128), F32), vmem((2, 4, 128), F32),
            vmem((2, 9, 128, 128), F32), vmem((RI, 128, 128), F32),
            vmem((128, 2, 7, 128), BF16), vmem((896, 128), F32),
            vmem((2, 512, 256), BF16), vmem((2, 3, 128, 128), F32),
            vmem((2, 128, 128), F32), vmem((2, 128, 128), F32), vmem((2, 128, 128), F32),
            vmem((2, 128, 128), BF16), vmem((2, 128, 128), BF16),
            vmem((128, 128), F32), vmem((128, 128), F32),
            vmem((2, 2, 3, 128, 128), BF16), vmem((2, 2, 3, 128, 128), BF16),
            dma((8,)), dma(()), dma((4, 3)), dma((4, 3)),
            dma((2,)), dma((2,)), dma((2,)), dma((2,)), dma((2, 2)), dma((2, 2)), dma(()),
        ],
        compiler_params=pltpu.CompilerParams(
            collective_id=0, has_side_effects=True, vmem_limit_bytes=60 << 20
        ),
    )(state, edge_metric, stencil_coef, norm_gain, biases, weights)


def solution(mesh):
    in_specs = (
        P("lat", "lon", None),
        P(None, "lat", "lon"),
        P(),
        P(),
        P(),
        P(None, ("lat", "lon"), None),
    )
    return jax.shard_map(
        on_device, mesh=mesh, in_specs=in_specs, out_specs=P("lat", "lon", None), check_vma=False
    )
```

time: 351 us -> 81.5 us (0.23); the launches traced: 345 us -> 81.3 us
  blocking collectives: 181 us -> 0 us
  other arithmetic: 75.8 us -> 0 us
  Pallas kernels: 0 us -> 73.9 us
  matrix products: 56.3 us -> 0 us
  starting transfers between devices: 12.5 us -> 0 us
  waiting for transfers between devices: 11.3 us -> 0 us
    all_gather x1 -> x0, blocking collectives: 181 us -> none  [on_device(): gathered = lax.all_gather(weights, ('lat', 'lon'), axis=1, tiled=True)]
    pallas_call x0 -> x1, Pallas kernels: none -> 73.9 us  [on_device(): pl.pallas_call(kernel, out_shape=jax.ShapeDtypeStruct(cube, BF16), in_spe...]
    dot_general x14 -> x0, matrix products: 56.3 us -> none  [the longest x2 21.6 us: grid_update(): jnp.dot(hidden, mats[6], preferred_element_type=jnp.float32)]
    reduce_sum x2 -> x0, other arithmetic: 47.6 us -> none  [grid_update(): jnp.mean(summed * summed, axis=-1, keepdims=True) + EPSILON]
    concatenate x4 -> x0, other arithmetic: 17.2 us -> none  [the longest x2 16.4 us: place_poles(): return jnp.concatenate([north[None], tall[1:-1], south[None]], axis=0)]
    ppermute x10 -> x0, starting transfers between devices: 12.5 us -> none  [the longest x4 8.23 us: extended(): lax.ppermute(tail, axis, [(i, (i + 1) % count) for i in range(ends)])]
    ppermute x10 -> x0, waiting for transfers between devices: 11.3 us -> none  [the longest x4 8.57 us: extended(): lax.ppermute(head, axis, [((i + 1) % count, i) for i in range(ends)])]
    convert_element_type x2 -> x0, other arithmetic: 9.45 us -> none  [grid_update(): normed = (summed * scale * gain).astype(jnp.bfloat16).reshape(-1, channels)]
  transfers between devices with their start and end apart: 10 -> 0, of which waited for: 5 -> 0; matrix products, arithmetic and copies ran while one was open for 2% -> 0% of each run, Pallas kernels for 0% -> 0%
where the time goes in v1:
time: 81.5 us; the launch traced here: 81.3 us
  Pallas kernels  73.9 us (91%)
  local copies, waits for them, and re-layouts  7.38 us (9%)
    pallas_call x1, Pallas kernels, on_device(): pl.pallas_call(kernel, out_shape=jax.ShapeDtypeStruct(cube, BF16), in_spe...  73.9 us
    unnamed x3, local copies, waits for them, and re-layouts  7.38 us

profile of v1, /device:TPU:1, one launch (start us, length us, event | category | flops | bytes accessed | tf_op | source)
XLA Modules:
  0.0 81.3 jit_solution(16395481227103312268)
XLA Ops:
  0.0 1.3 %copy.8.w_h = bf16[2,7,128]{2,1,0:T(8,128)(2,1)} copy(bf16[2,7,128]{2,0,1:T(2,128)(2,1)} %param.11) | data formatting | bytes 7168 | tf_op args[5]
  1.3 1.3 %copy.7.coef_h = f32[2,9,128]{2,1,0:T(8,128)} copy(f32[2,9,128]{2,0,1:T(2,128)} %param.8) | data formatting | bytes 18432 | tf_op args[2]
  2.6 73.9 %shard_map.64 = bf16[128,128,128]{2,1,0:T(8,128)(2,1)} custom-call(bf16[128,128,128]{2,1,0:T(8,128)(2,1)} %state.1, f32[9,128,128]{2,1,0:T(8,128)} %met_h.1, f32[2,9,128]{2,1,0:T(8,128)} %copy.7.coef_h, f32[2,128]{1,0:T(2,128)} %gain_h.1, f32[2,4,128]{2,1,0:T(4,128)} %bias_h.1, bf16[2,7,128]{2,1,0:T(8,128)(2,1)} %copy.8.w_h), custom_call_target="tpu_custom_call" | custom-call | tf_op jit(solution)/shard_map/pallas_call | solution.py:380
  76.5 4.8 %copy.10 = bf16[128,128,128]{2,1,0:T(8,128)(2,1)} copy(bf16[128,128,128]{2,1,0:T(8,128)(2,1)} %shard_map.64) | data formatting | bytes 8388608

commit v2 on v1

--- a/solution.py
+++ b/solution.py
@@ -45,12 +45,12 @@
         nrm[i0 + r] = (agg[r] * scale).astype(BF16)
 
 
-def gate_block(i0, nrm, xc, wt, bias, t, emit):
+def gate_block(i0, nrm, hb, xc, wt, bias, t, emit):
     h = [xc[i0 + 1 + r] for r in range(RG)]
     z = jnp.concatenate(
         [
             jnp.concatenate([nrm[i0 + r] for r in range(RG)], axis=1),
-            jnp.concatenate([v.astype(BF16) for v in h], axis=1),
+            jnp.concatenate([hb[i0 + r] for r in range(RG)], axis=1),
         ],
         axis=0,
     )
@@ -75,10 +75,14 @@
     return (y * 2 + z % 2) * 16 + (z // 2) * 8 + x * 2 + core
 
 
-def prepare_weights(t, wg, w32, gain, bvec, wt, bias):
+def unpack_weights(wg, w32):
     for s in range(128):
-        w32[pl.ds(7 * slot_owner(s), 7), :] = wg[s, t].astype(F32)
-    mt = [w32[128 * k : 128 * k + 128, :].T.astype(BF16) for k in range(7)]
+        for q in range(7):
+            w32[pl.ds(14 * slot_owner(s) + 2 * q, 2), :] = wg[s, q].astype(F32)
+
+
+def prepare_weights(t, w32, gain, bvec, wt, bias):
+    mt = [w32[pl.ds(256 * k + t, 128, stride=2), :].T.astype(BF16) for k in range(7)]
     grow = gain[t : t + 1, :]
     column = lambda k: jnp.broadcast_to(bvec[t, k : k + 1, :], (128, 128)).T
     b0 = column(0)
@@ -105,9 +109,9 @@
 
 def kernel(
     state, met_h, coef_h, gain_h, bias_h, w_h, out,
-    xnat, xl, xc, xr, nrm, stage, met, coef_v, gain, bvec, coef, agg, wg, w32, wt, bias,
-    gnat, gnat_r, gacc, gsend, grecv, gw, ge, rsend, rrecv,
-    in_sem, w_sem, ag_send, ag_recv, gn_send, gn_recv, gb_send, gb_recv, rr_send, rr_recv, out_sem,
+    xnat, hb, xl, xc, xr, nrm, met, coef_v, gain, bvec, coef, agg, wg, w32, wt, bias,
+    gnat, gnat_r, gacc, gsend, grecv, gh, shift, rsend, rrecv,
+    in_sem, w_sem, ag_send, ag_recv, gn_send, gn_recv, gb_send, gb_recv, rr_send, rr_recv,
 ):
     lat, lon = lax.axis_index("lat"), lax.axis_index("lon")
     y, z_lo = lat // 2, lat % 2
@@ -219,82 +223,93 @@
             device_id=target, device_id_type=MESH,
         )
 
-    first_sides = [
-        side(gnat.at[0], gnat_r.at[0], gn_send.at[0], gn_recv.at[0], west),
-        side(gnat.at[1], gnat_r.at[1], gn_send.at[1], gn_recv.at[1], east),
-    ]
+    first_sides = []
+    for half in (0, 1):
+        mine = pl.ds(64 * half, 64)
+        for k, target in ((0, west), (1, east)):
+            first_sides.append(
+                side(
+                    gnat.at[k, mine], gnat_r.at[half, pl.ds(64 - 64 * k, 64)],
+                    gn_send.at[half, k], gn_recv.at[half, k], target,
+                )
+            )
     start_all(first_sides)
+    def turn(s, carry):
+        for k in range(8):
+            i = s * 8 + k
+            v = xnat[i].T
+            hb[i] = v
+            xc[i + 1] = v.astype(F32)
+        return carry
+
+    lax.fori_loop(0, ROWS // 8, turn, 0)
     wait_stage(along_x)
     along_z = stage_copies(1)
     start_all(along_z[0])
-
-    def turn(s, carry):
-        for k in range(8):
-            i = s * 8 + k
-            xc[i + 1] = xnat[i].T.astype(F32)
-        return carry
-
-    lax.fori_loop(0, ROWS // 16, turn, 0)
-    wait_stage(along_z)
-    along_y = stage_copies(2)
-    start_all(along_y[0])
-    lax.fori_loop(ROWS // 16, ROWS // 8, turn, 0)
 
     for copy in smalls:
         copy.wait()
     for t in range(2):
         for d in range(9):
-            coef[t, d] = jnp.broadcast_to(coef_v[t, d : d + 1, :], (128, 128)).T
+            coef[t, d] = jnp.broadcast_to(coef_v[d, t : t + 1, :], (128, 128)).T
 
     for copy in first_sides:
         copy.wait()
-    ge[...] = gnat_r[0].T
-    gw[...] = pltpu.roll(gnat_r[1].T, 127, 1)
-    wait_stage(along_y)
-    other = 1 - core
-    across = (
-        [hop(3, 0, 64, core * 64, place(y, z, x, other))],
-        [hop(3, 0, 64, other * 64, place(y, z, x, other))],
-    )
-    start_all(across[0])
-
-    lane8 = lane_iota((8, 128))
-
-    def build_row(i):
-        left_shift, right_shift = (129 - i) % 128, 127 - i
-        for cb in range(16):
-            cs = slice(8 * cb, 8 * cb + 8)
-            v = xc[i + 1, cs, :]
-            xl[i + 1, cs, :] = jnp.where(
-                lane8 == 0, pltpu.roll(gw[cs, :], left_shift, 1), pltpu.roll(v, 1, 1)
-            )
-            xr[i + 1, cs, :] = jnp.where(
-                lane8 == 127, pltpu.roll(ge[cs, :], right_shift, 1), pltpu.roll(v, 127, 1)
-            )
-
-    def stencil_phase(t):
-        def early(s, carry):
-            build_row(jnp.where(s == 0, 127, s - 1))
-            return carry
-
-        lax.fori_loop(0, 10, early, 0)
-        for edge, row in ((0, 1), (1, ROWS)):
+    for half in (0, 1):
+        gh[half] = gnat_r[half].T
+
+    src = lax.broadcasted_iota(jnp.int32, (256, 256), 0)
+    dst = lax.broadcasted_iota(jnp.int32, (256, 256), 1)
+    to_left, to_right = dst < 128, dst >= 128
+    moved = (src < 128) & ((to_left & (dst == src + 1)) | (to_right & (dst == src + 127)))
+    ghost = (src >= 128) & ((src < 192) & (dst == 0) | (src >= 192) & (dst == 255))
+    shift[...] = jnp.where(moved | ghost, 1.0, 0.0).astype(BF16)
+    lane_row = lane_iota((1, 128)) % 64
+
+    def build(block):
+        i0 = block * RI
+        parts = []
+        for r in range(RI):
+            i = i0 + r
+            mask = jnp.where(lane_row == i % 64, 1.0, 0.0)
+            ghosts = (gh[i // 64] * mask).astype(BF16)
+            parts.append(jnp.concatenate([hb[i], ghosts], axis=1))
+        both = jnp.dot(jnp.concatenate(parts, axis=0), shift[...], preferred_element_type=F32)
+        for r in range(RI):
+            xl[i0 + r + 1] = both[128 * r : 128 * r + 128, :128]
+            xr[i0 + r + 1] = both[128 * r : 128 * r + 128, 128:]
+
+    last_block = ROWS // RI - 1
+
+    def stencil_phase(t, hooks):
+        def start_edge(edge, row):
             for part, ref in enumerate((xl, xc, xr)):
                 rsend[t, edge, part] = ref[row].astype(BF16)
-        rows = [
-            side(rsend.at[t, 0], rrecv.at[t, north_slot], rr_send.at[t, 0], rr_recv.at[t, north_slot], north),
-            side(rsend.at[t, 1], rrecv.at[t, south_slot], rr_send.at[t, 1], rr_recv.at[t, south_slot], south),
-        ]
-        start_all(rows)
+            slot, target = ((north_slot, north), (south_slot, south))[edge]
+            copy = side(
+                rsend.at[t, edge], rrecv.at[t, slot], rr_send.at[t, edge], rr_recv.at[t, slot], target
+            )
+            copy.start()
+            return copy
+
+        for block in range(3):
+            build(block)
+        rows = [start_edge(0, 1)]
 
         def inner(s, carry):
-            i0 = s * RI
-            stencil_block(i0, xl, xc, xr, met, coef, t, agg, nrm)
-            for k in range(RI):
-                build_row(jnp.minimum(i0 + RI + 1 + k, 127))
+            stencil_block(s * RI, xl, xc, xr, met, coef, t, agg, nrm)
+            build(jnp.minimum(s + 2, last_block))
             return carry
 
-        lax.fori_loop(1, ROWS // RI - 1, inner, 0)
+        at = 1
+        for stop in sorted(hooks):
+            lax.fori_loop(at, stop, inner, 0)
+            at = stop
+            hooks[stop]()
+            if stop == 14:
+                build(last_block)
+                rows.append(start_edge(1, ROWS))
+        lax.fori_loop(at, last_block, inner, 0)
         for copy in rows:
             copy.wait_send()
         for edge, target in ((0, north), (1, south)):
@@ -311,11 +326,27 @@
 
         lax.fori_loop(0, 2, outer, 0)
 
-    stencil_phase(0)
+    along_y, across = stage_copies(2), None
+    other = 1 - core
+    across = (
+        [hop(3, 0, 64, core * 64, place(y, z, x, other))],
+        [hop(3, 0, 64, other * 64, place(y, z, x, other))],
+    )
+
+    def z_done():
+        wait_stage(along_z)
+        start_all(along_y[0])
+
+    def y_done():
+        wait_stage(along_y)
+        start_all(across[0])
+
+    stencil_phase(0, {8: z_done, 14: lambda: None, 25: y_done})
 
     wait_stage(across)
+    unpack_weights(wg, w32)
     for t in range(2):
-        prepare_weights(t, wg, w32, gain, bvec, wt, bias)
+        prepare_weights(t, w32, gain, bvec, wt, bias)
 
     lane16 = lane_iota((16, 128))
 
@@ -327,6 +358,7 @@
             for r in range(RG):
                 i = i0 + r
                 v = outs[r].astype(F32)
+                hb[i, cs, :] = outs[r]
                 xc[i + 1, cs, :] = v
                 turned = pltpu.roll(v, i, 1)
                 head = jnp.where(lane16 == i, turned, head)
@@ -334,23 +366,33 @@
             gacc[0, cs, :] = head
             gacc[1, cs, :] = tail
 
-        gate_block(i0, nrm, xc, wt, bias, 0, emit)
+        gate_block(i0, nrm, hb, xc, wt, bias, 0, emit)
         return carry
 
     gacc[...] = jnp.zeros_like(gacc)
-    lax.fori_loop(0, ROWS // RG, gates_first, 0)
-    gsend[...] = gacc[...].astype(BF16)
     second_sides = [
-        side(gsend.at[0], grecv.at[0], gb_send.at[0], gb_recv.at[0], west),
-        side(gsend.at[1], grecv.at[1], gb_send.at[1], gb_recv.at[1], east),
+        [
+            side(gsend.at[half, k], grecv.at[half, k], gb_send.at[half, k], gb_recv.at[half, k], target)
+            for k, target in ((0, west), (1, east))
+        ]
+        for half in (0, 1)
     ]
-    start_all(second_sides)
-    for copy in second_sides:
-        copy.wait()
-    ge[...] = grecv[0].astype(F32)
-    gw[...] = grecv[1].astype(F32)
-
-    stencil_phase(1)
+    for half in (0, 1):
+        lax.fori_loop(half * ROWS // RG // 2, (half + 1) * ROWS // RG // 2, gates_first, 0)
+        gsend[half] = gacc[...].astype(BF16)
+        start_all(second_sides[half])
+
+    low = lane_iota((128, 128)) < 64
+
+    def take_sides(half):
+        for copy in second_sides[half]:
+            copy.wait()
+        from_east = pltpu.roll(grecv[half, 0].astype(F32), 64 - 64 * half, 1)
+        from_west = pltpu.roll(grecv[half, 1].astype(F32), 1 + 64 * half, 1)
+        gh[half] = jnp.where(low, from_west, from_east)
+
+    take_sides(0)
+    stencil_phase(1, {14: lambda: take_sides(1)})
 
     def gates_second(s, carry):
         i0 = s * RG
@@ -360,16 +402,12 @@
             for r in range(RG):
                 kept[r].append(outs[r])
 
-        gate_block(i0, nrm, xc, wt, bias, 1, emit)
+        gate_block(i0, nrm, hb, xc, wt, bias, 1, emit)
         for r in range(RG):
-            stage[i0 + r] = jnp.concatenate(kept[r], axis=0).T
-        pltpu.make_async_copy(
-            stage.at[pl.ds(i0, RG)], out.at[pl.ds(i0, RG)], out_sem
-        ).start()
+            out[i0 + r] = jnp.concatenate(kept[r], axis=0).T
         return carry
 
     lax.fori_loop(0, ROWS // RG, gates_second, 0)
-    pltpu.make_async_copy(stage, out, out_sem).wait()
 
 
 def on_device(state, edge_metric, stencil_coef, norm_gain, biases, weights):
@@ -379,27 +417,34 @@
     dma, vmem = pltpu.SemaphoreType.DMA, pltpu.VMEM
     return pl.pallas_call(
         kernel,
-        out_shape=jax.ShapeDtypeStruct(cube, BF16),
+        out_shape=pltpu.VMEM(cube, BF16),
         in_specs=[anywhere] * 6,
-        out_specs=anywhere,
+        out_specs=pl.BlockSpec(memory_space=pltpu.VMEM),
         scratch_shapes=[
-            vmem(cube, BF16), vmem(tall, F32), vmem(tall, F32), vmem(tall, F32),
-            vmem(cube, BF16), vmem(cube, BF16),
-            vmem((9, 128, 128), F32), vmem((2, 9, 128), F32), vmem((2, 128), F32), vmem((2, 4, 128), F32),
+            vmem(cube, BF16), vmem(cube, BF16), vmem(tall, F32), vmem(tall, F32), vmem(tall, F32),
+            vmem(cube, BF16),
+            vmem((9, 128, 128), F32), vmem((9, 2, 128), F32), vmem((2, 128), F32), vmem((2, 4, 128), F32),
             vmem((2, 9, 128, 128), F32), vmem((RI, 128, 128), F32),
-            vmem((128, 2, 7, 128), BF16), vmem((896, 128), F32),
+            vmem((128, 7, 2, 128), BF16), vmem((1792, 128), F32),
             vmem((2, 512, 256), BF16), vmem((2, 3, 128, 128), F32),
             vmem((2, 128, 128), F32), vmem((2, 128, 128), F32), vmem((2, 128, 128), F32),
-            vmem((2, 128, 128), BF16), vmem((2, 128, 128), BF16),
-            vmem((128, 128), F32), vmem((128, 128), F32),
+            vmem((2, 2, 128, 128), BF16), vmem((2, 2, 128, 128), BF16),
+            vmem((2, 128, 128), F32), vmem((256, 256), BF16),
             vmem((2, 2, 3, 128, 128), BF16), vmem((2, 2, 3, 128, 128), BF16),
             dma((8,)), dma(()), dma((4, 3)), dma((4, 3)),
-            dma((2,)), dma((2,)), dma((2,)), dma((2,)), dma((2, 2)), dma((2, 2)), dma(()),
+            dma((2, 2)), dma((2, 2)), dma((2, 2)), dma((2, 2)), dma((2, 2)), dma((2, 2)),
         ],
         compiler_params=pltpu.CompilerParams(
-            collective_id=0, has_side_effects=True, vmem_limit_bytes=60 << 20
+            collective_id=0, has_side_effects=True, vmem_limit_bytes=50 << 20
         ),
-    )(state, edge_metric, stencil_coef, norm_gain, biases, weights)
+    )(
+        state,
+        edge_metric,
+        jnp.transpose(stencil_coef, (1, 0, 2)),
+        norm_gain,
+        biases,
+        jnp.transpose(weights, (1, 0, 2)),
+    )
 
 
 def solution(mesh):

time: 81.5 us -> 64.7 us (0.79)
  Pallas kernels: 73.9 us -> 62.5 us
  local copies, waits for them, and re-layouts: 7.38 us -> 2.02 us
    pallas_call x1, Pallas kernels: 73.9 us -> 62.5 us  [on_device(): pl.pallas_call(kernel, out_shape=pltpu.VMEM(cube, BF16), in_specs=[anywhe...]
    unnamed x3 -> x1, local copies, waits for them, and re-layouts: 7.38 us -> 2.02 us
where the time goes in v2:
time: 64.7 us; the launch traced here: 64.5 us
  Pallas kernels  62.5 us (97%)
  local copies, waits for them, and re-layouts  2.02 us (3%)
    pallas_call x1, Pallas kernels, on_device(): pl.pallas_call(kernel, out_shape=pltpu.VMEM(cube, BF16), in_specs=[anywhe...  62.5 us
    unnamed x1, local copies, waits for them, and re-layouts  2.02 us

profile of v2, /device:TPU:1, one launch (start us, length us, event | category | flops | bytes accessed | tf_op | source)
XLA Modules:
  0.0 64.5 jit_solution(8668726900334554694)
XLA Ops:
  0.0 62.5 %shard_map.64 = bf16[128,128,128]{2,1,0:T(8,128)(2,1)S(1)} custom-call(bf16[128,128,128]{2,1,0:T(8,128)(2,1)} %state.1, f32[9,128,128]{2,1,0:T(8,128)} %met_h.1, f32[9,2,128]{2,1,0:T(2,128)} %bitcast.2, f32[2,128]{1,0:T(2,128)} %gain_h.1, f32[2,4,128]{2,1,0:T(4,128)} %bias_h.1, bf16[7,2,128]{2,1,0:T(2,128)(2,1)} %bitcast.3), custom_call_target="tpu_custom_call" | custom-call | tf_op jit(solution)/shard_map/pallas_call | solution.py:418
  62.5 2.0 %copy.8 = bf16[128,128,128]{2,1,0:T(8,128)(2,1)} copy(bf16[128,128,128]{2,1,0:T(8,128)(2,1)S(1)} %shard_map.64) | data formatting | bytes 8388608
